TPU v7x, 128 devices: a whole 4x4x4 slice. The times are simulated.
128 devices in a mesh: seq: 32 (over z, y, core), mp: 4 (over x).
Axes of the slice: x: 4, y: 4, z: 4, core: 2. Of those that a mesh axis runs over, the one named last changes fastest.
Arguments:
- token_ids: int32 [2, 4096], P(None, 'seq'), may hold values from 0 to 511, as said below
- pair_mask: int32 [4096], P('seq'), may hold values from 0 to 1
- embed_table: bfloat16 [512, 3, 4096], P(None, None, 'mp'), may hold values from -6 to 6
- conv_filter: bfloat16 [256, 128], P('mp'), may hold values from -0.9 to 1
- w_out: bfloat16 [4096, 4096], P('mp'), may hold values from -0.09375 to 0.09375
- w_qkv: bfloat16 [3, 32, 128, 128], P(None, 'mp'), may hold values from -0.61871843 to 0.61871843
Outputs:
- gram: float32 [32, 128, 128], P('mp', 'seq')
Inputs may be any that keep to these rules, and one draw needn't show every extreme that they name: `token_ids`: row 1 equals row 0 at about half of the positions.
All inputs are finite; a program needn't handle non-finite values.
Results may differ from a plain program's by a relative error of at most 0.0074.
Values may be sent and summed in bfloat16 or wider, within the bound.
A program may use at most 128 MiB of HBM per device.

v0:
```python
import math

import jax
import jax.numpy as jnp
from jax import lax
from jax.sharding import PartitionSpec as P

MASKED_SCORE = -1e30


def from_behind(value, axis, steps):
    count = lax.axis_size(axis)
    initial, last = (max(0, -steps), min(count, count - steps))
    return lax.ppermute(value, axis, [(source, source + steps) for source in range(initial, last)])


def lookup(token_ids, embed_table):
    vocab_size = embed_table.shape[0]
    onehot = (
        token_ids[:, :, None] == jnp.arange(vocab_size, dtype=jnp.int32)[None, None, :]
    ).astype(jnp.bfloat16)
    flat_table = embed_table.reshape(vocab_size, -1)
    features = jnp.einsum("stv,vc->stc", onehot, flat_table, preferred_element_type=jnp.float32)
    return features.astype(jnp.bfloat16).reshape(
        token_ids.shape[0], token_ids.shape[1], 3, embed_table.shape[2]
    )


def toeplitz(conv_filter):
    tap_count = conv_filter.shape[1]
    out_index = jnp.arange(tap_count, dtype=jnp.int32)[:, None, None]
    in_index = jnp.arange(2 * tap_count, dtype=jnp.int32)[None, :, None]
    lag_index = jnp.arange(tap_count, dtype=jnp.int32)[None, None, :]
    selector = (lag_index == out_index + tap_count - in_index).astype(jnp.bfloat16)
    return jnp.einsum(
        "gj,tsj->gts", conv_filter, selector, preferred_element_type=jnp.float32
    ).astype(jnp.bfloat16)


def project(row_block, weight):
    return jnp.einsum(
        "sthd,hde->sthe", row_block, weight, preferred_element_type=jnp.float32
    ).astype(jnp.bfloat16)


def body(token_ids, pair_mask, embed_table, conv_filter, w_out, w_qkv):
    local_len = token_ids.shape[1]
    channels = embed_table.shape[2]
    filters, tap_count = conv_filter.shape
    group_width = channels // filters
    head_count, head_dim = (w_qkv.shape[1], w_qkv.shape[2])
    my_index = lax.axis_index("seq")
    score_scale = 1.0 / math.sqrt(head_dim)
    features = lookup(token_ids, embed_table)
    gated = (features[:, :, 1].astype(jnp.float32) * features[:, :, 2].astype(jnp.float32)).astype(
        jnp.bfloat16
    )
    before = from_behind(gated, "seq", 1)
    window = jnp.concatenate([before, gated], axis=1)
    blocks = local_len // tap_count
    lower_half = window[:, :local_len].reshape(2, blocks, tap_count, filters, group_width)
    upper_half = window[:, tap_count:].reshape(2, blocks, tap_count, filters, group_width)
    framed = jnp.concatenate([lower_half, upper_half], axis=2)
    convolved = jnp.einsum(
        "gts,bnsgc->bntgc", toeplitz(conv_filter), framed, preferred_element_type=jnp.float32
    )
    hyena_out = (
        features[:, :, 0].astype(jnp.float32) * convolved.reshape(2, local_len, channels)
    ).astype(jnp.bfloat16)
    partial_value = jnp.dot(
        hyena_out.reshape(2 * local_len, channels), w_out, preferred_element_type=jnp.float32
    )
    partial_value = partial_value.reshape(2, local_len, w_out.shape[1])
    mixed_out = lax.psum_scatter(partial_value, "mp", scatter_dimension=2, tiled=True).astype(
        jnp.bfloat16
    )
    mixed_heads = mixed_out.reshape(2, local_len, head_count, head_dim)
    queries = project(mixed_heads, w_qkv[0])
    query_pos = my_index * local_len + jnp.arange(local_len, dtype=jnp.int32)

    def fold_block(running, key_rows, value_rows, offset):
        row_max, row_sum, weighted = running
        scores = (
            jnp.einsum("sqhe,skhe->shqk", queries, key_rows, preferred_element_type=jnp.float32)
            * score_scale
        )
        key_pos = offset + jnp.arange(key_rows.shape[1], dtype=jnp.int32)
        causal = key_pos[None, :] <= query_pos[:, None]
        new_max = jnp.maximum(row_max, jnp.max(jnp.where(causal, scores, MASKED_SCORE), axis=-1))
        weights = jnp.where(causal, jnp.exp(scores - new_max[..., None]), 0.0)
        rescale = jnp.exp(row_max - new_max)
        row_sum = row_sum * rescale + jnp.sum(weights, axis=-1)
        update = jnp.einsum(
            "shqk,skhe->shqe",
            weights.astype(jnp.bfloat16),
            value_rows,
            preferred_element_type=jnp.float32,
        )
        weighted = weighted * rescale[..., None] + update
        return (new_max, row_sum, weighted)

    initial = (
        jnp.full((2, head_count, local_len), MASKED_SCORE, jnp.float32),
        jnp.zeros((2, head_count, local_len), jnp.float32),
        jnp.zeros((2, head_count, local_len, head_dim), jnp.float32),
    )
    key_heads = project(mixed_heads, w_qkv[1])
    value_heads = project(mixed_heads, w_qkv[2])

    def expand_pair(pieces):
        return (pieces[0], pieces[1])

    pieces = (
        lax.all_gather(key_heads, "seq", axis=1, tiled=True),
        lax.all_gather(value_heads, "seq", axis=1, tiled=True),
    )
    row_count = pieces[0].shape[1]
    block_rows = 1024

    def advance(block_index, state_now):
        offset = block_index * block_rows
        sliced = tuple(
            (lax.dynamic_slice_in_dim(member, offset, block_rows, 1) for member in pieces)
        )
        key_rows, value_rows = expand_pair(sliced)
        return fold_block(state_now, key_rows, value_rows, offset)

    final = lax.fori_loop(0, row_count // block_rows, advance, initial)
    row_max, row_sum, weighted = final
    attended = weighted / row_sum[..., None]
    difference = (attended[0] - attended[1]).astype(jnp.bfloat16)
    mask_float = pair_mask.astype(jnp.bfloat16)
    kept_rows = difference * mask_float[None, :, None]
    partial_gram = jnp.einsum(
        "hte,htf->hef", kept_rows, difference, preferred_element_type=jnp.float32
    )
    gram_sum = lax.psum_scatter(partial_gram, "seq", scatter_dimension=1, tiled=True)
    kept_count = lax.psum(jnp.sum(pair_mask.astype(jnp.float32)), "seq")
    return gram_sum / jnp.maximum(kept_count, 1.0)


def solution(mesh):
    in_specs = (
        P(None, "seq"),
        P("seq"),
        P(None, None, "mp"),
        P("mp", None),
        P("mp", None),
        P(None, "mp", None, None),
    )
    out_specs = P("mp", "seq", None)
    return jax.shard_map(body, mesh=mesh, in_specs=in_specs, out_specs=out_specs, check_vma=False)
```

profile of v0, /device:TPU:1, one launch (start us, length us, event | category | flops | bytes accessed | tf_op | source)
XLA Modules:
  0.0 409.1 jit_solution(17363381717655313146)
XLA Ops:
  18.9 9.1 %convert_bitcast_fusion = bf16[64,128,256,1]{2,0,1,3:T(8,128)(2,1)} fusion(s32[128,256]{1,0:T(8,128)S(1)} %iota_subtract_fusion, bf16[64,128]{1,0:T(8,128)(2,1)S(1)} %copy-done), kind=kOutput, calls=%fused_computation.36 | convolution fusion | flops 543162368 | bytes 4341760 | tf_op jit(solution)/shard_map/gj,tsj->gts/dot_general | solution.py:35
  33.0 7.7 %fusion.25 = f32[2,128,4096]{2,1,0:T(8,128)} fusion(bf16[1024,4096]{1,0:T(8,128)(2,1)} %param.12, f32[2,128,1024]{1,2,0:T(8,128)S(1)} %bitcast.104, bf16[2,128,3,1024]{1,3,2,0:T(8,128)(2,1)S(1)} %bitcast.103), kind=kOutput, calls=%fused_computation.31 | convolution fusion | flops 2148270080 | bytes 14155776 | tf_op jit(solution)/shard_map/dot_general | solution.py:70
  40.8 48.5 %reduce-scatter.3.cloned.1.call-done = f32[2,128,1024]{2,1,0:T(8,128)} async-done(((f32[2,128,4096]{2,1,0:T(8,128)}), f32[2,128,1024]{2,1,0:T(8,128)}) %reduce-scatter.3.cloned.1.call-update) | async-done | bytes 1048592 | tf_op jit(solution)/shard_map/reduce_scatter | solution.py:74
  94.8 69.8 %all-gather.3.cloned.1.call-done = bf16[2,4096,8,128]{3,1,0,2:T(8,128)(2,1)} async-done(((bf16[2,128,8,128]{3,1,0,2:T(8,128)(2,1)}), bf16[2,4096,8,128]{3,1,0,2:T(8,128)(2,1)}) %all-gather.3.cloned.1.call-update) | async-done | bytes 16777232 | tf_op jit(solution)/shard_map/all_gather | solution.py:114
  164.6 74.6 %all-gather.5.cloned.1.call-done = bf16[2,4096,8,128]{3,1,0,2:T(8,128)(2,1)} async-done(((bf16[2,128,8,128]{3,1,0,2:T(8,128)(2,1)}), bf16[2,4096,8,128]{3,1,0,2:T(8,128)(2,1)}) %all-gather.5.cloned.1.call-update) | async-done | bytes 16777232 | tf_op jit(solution)/shard_map/all_gather | solution.py:115
  239.2 85.7 %while.18 = (s32[]{:T(128)}, f32[2,8,128]{2,1,0:T(8,128)S(1)}, f32[2,8,128]{2,1,0:T(8,128)S(1)}, f32[2,8,128,128]{3,2,1,0:T(8,128)S(1)}, bf16[2,4096,8,128]{3,1,...) while((s32[]{:T(128)}, f32[2,8,128]{2,1,0:T(8,128)S(1)}, ...), condition=%wide.region_4.5_spmd.clone, body=%wide.region_1.4_spmd.clone.sunk | while | flops 1097739392 | bytes 87172312 | solution.py:128
  239.2 6.2 %constant_dynamic-slice_fusion.3 = (bf16[2,1024,8,128]{3,1,0,2:T(8,128)(2,1)}, bf16[2,1024,8,128]{3,1,0,2:T(8,128)(2,1)S(1)}) fusion(bf16[2,4096,8,128]{3,1,0,2:T(8,128)(2,1)} %get-tuple-element.314, s32[]{:T(128)S(6)} %select_n.44, bf16[2,4096,8,128]{3,1,0,2:T(8,128)(2,1)} %get-tuple-element.312), kind=kLoop, calls=%fused_computation.25.clone.1 | loop fusion | bytes 16777220 | tf_op jit(solution)/shard_map/while/body/eval_jaxpr/dynamic_slice | solution.py:123
  245.6 4.6 %fusion.72 = (f32[2,8,128]{2,1,0:T(8,128)S(1)}, f32[2,8,1024,128]{3,2,1,0:T(8,128)}) fusion(pred[128,1024]{0,1:T(8,128)(4,1)S(1)} %broadcast_compare_fusion.2, bf16[2,128,8,128]{3,1,2,0:T(8,128)(2,1)S(1)} %get-tuple-element.313, bf16[2,1024,8,128]{3,1,0,2:T(8,128)(2,1)S(1)} %get-tuple-element.278), kind=kOutput, calls=%fused_computation.3.clone.1 | convolution fusion | flops 543160320 | bytes 13246464 | tf_op jit(solution)/shard_map/while/body/eval_jaxpr/sqhe,skhe->shqk/dot_general | solution.py:84
  250.3 5.2 %fusion.73 = f32[2,8,128]{2,1,0:T(8,128)S(1)} fusion(f32[2,8,1024,128]{3,2,1,0:T(8,128)} %get-tuple-element.280, f32[2,8,128]{2,1,0:T(8,128)S(1)} %select_maximum_fusion.2, pred[128,1024]{0,1:T(8,128)(4,1)S(1)} %broadcast_compare_fusion.2), kind=kLoop, calls=%fused_computation.7.clone.1 | loop fusion | flops 8386560 | bytes 8536064 | tf_op jit(solution)/shard_map/while/body/eval_jaxpr/reduce_sum | solution.py:92
  256.0 4.6 %fusion.75 = f32[2,8,128,128]{3,2,1,0:T(8,128)S(1)} fusion(bf16[2,1024,8,128]{3,1,0,2:T(8,128)(2,1)} %get-tuple-element.282, f32[2,8,1024,128]{3,2,1,0:T(8,128)S(1)} %copy-done.2, f32[2,8,128]{2,1,0:T(8,128)S(1)} %select_maximum_fusion.2, pred[128,1024]{0,1:T(8,128)(4,1)S(1)} %broadcast_compare_fusion.2, ...), kind=kOutput, calls=%fused_computation.16.clone.1 | convolution fusion | flops 546045952 | bytes 14827521 | tf_op jit(solution)/shard_map/while/body/eval_jaxpr/shqk,skhe->shqe/dot_general | solution.py:93
  260.7 6.2 %constant_dynamic-slice_fusion.3 = (bf16[2,1024,8,128]{3,1,0,2:T(8,128)(2,1)}, bf16[2,1024,8,128]{3,1,0,2:T(8,128)(2,1)S(1)}) fusion(bf16[2,4096,8,128]{3,1,0,2:T(8,128)(2,1)} %get-tuple-element.314, s32[]{:T(128)S(6)} %select_n.44, bf16[2,4096,8,128]{3,1,0,2:T(8,128)(2,1)} %get-tuple-element.312), kind=kLoop, calls=%fused_computation.25.clone.1 | loop fusion | bytes 16777220 | tf_op jit(solution)/shard_map/while/body/eval_jaxpr/dynamic_slice | solution.py:123
  267.1 4.6 %fusion.72 = (f32[2,8,128]{2,1,0:T(8,128)S(1)}, f32[2,8,1024,128]{3,2,1,0:T(8,128)}) fusion(pred[128,1024]{0,1:T(8,128)(4,1)S(1)} %broadcast_compare_fusion.2, bf16[2,128,8,128]{3,1,2,0:T(8,128)(2,1)S(1)} %get-tuple-element.313, bf16[2,1024,8,128]{3,1,0,2:T(8,128)(2,1)S(1)} %get-tuple-element.278), kind=kOutput, calls=%fused_computation.3.clone.1 | convolution fusion | flops 543160320 | bytes 13246464 | tf_op jit(solution)/shard_map/while/body/eval_jaxpr/sqhe,skhe->shqk/dot_general | solution.py:84
  271.7 5.2 %fusion.73 = f32[2,8,128]{2,1,0:T(8,128)S(1)} fusion(f32[2,8,1024,128]{3,2,1,0:T(8,128)} %get-tuple-element.280, f32[2,8,128]{2,1,0:T(8,128)S(1)} %select_maximum_fusion.2, pred[128,1024]{0,1:T(8,128)(4,1)S(1)} %broadcast_compare_fusion.2), kind=kLoop, calls=%fused_computation.7.clone.1 | loop fusion | flops 8386560 | bytes 8536064 | tf_op jit(solution)/shard_map/while/body/eval_jaxpr/reduce_sum | solution.py:92
  277.5 4.6 %fusion.75 = f32[2,8,128,128]{3,2,1,0:T(8,128)S(1)} fusion(bf16[2,1024,8,128]{3,1,0,2:T(8,128)(2,1)} %get-tuple-element.282, f32[2,8,1024,128]{3,2,1,0:T(8,128)S(1)} %copy-done.2, f32[2,8,128]{2,1,0:T(8,128)S(1)} %select_maximum_fusion.2, pred[128,1024]{0,1:T(8,128)(4,1)S(1)} %broadcast_compare_fusion.2, ...), kind=kOutput, calls=%fused_computation.16.clone.1 | convolution fusion | flops 546045952 | bytes 14827521 | tf_op jit(solution)/shard_map/while/body/eval_jaxpr/shqk,skhe->shqe/dot_general | solution.py:93
  282.1 6.2 %constant_dynamic-slice_fusion.3 = (bf16[2,1024,8,128]{3,1,0,2:T(8,128)(2,1)}, bf16[2,1024,8,128]{3,1,0,2:T(8,128)(2,1)S(1)}) fusion(bf16[2,4096,8,128]{3,1,0,2:T(8,128)(2,1)} %get-tuple-element.314, s32[]{:T(128)S(6)} %select_n.44, bf16[2,4096,8,128]{3,1,0,2:T(8,128)(2,1)} %get-tuple-element.312), kind=kLoop, calls=%fused_computation.25.clone.1 | loop fusion | bytes 16777220 | tf_op jit(solution)/shard_map/while/body/eval_jaxpr/dynamic_slice | solution.py:123
  288.5 4.6 %fusion.72 = (f32[2,8,128]{2,1,0:T(8,128)S(1)}, f32[2,8,1024,128]{3,2,1,0:T(8,128)}) fusion(pred[128,1024]{0,1:T(8,128)(4,1)S(1)} %broadcast_compare_fusion.2, bf16[2,128,8,128]{3,1,2,0:T(8,128)(2,1)S(1)} %get-tuple-element.313, bf16[2,1024,8,128]{3,1,0,2:T(8,128)(2,1)S(1)} %get-tuple-element.278), kind=kOutput, calls=%fused_computation.3.clone.1 | convolution fusion | flops 543160320 | bytes 13246464 | tf_op jit(solution)/shard_map/while/body/eval_jaxpr/sqhe,skhe->shqk/dot_general | solution.py:84
  293.2 5.2 %fusion.73 = f32[2,8,128]{2,1,0:T(8,128)S(1)} fusion(f32[2,8,1024,128]{3,2,1,0:T(8,128)} %get-tuple-element.280, f32[2,8,128]{2,1,0:T(8,128)S(1)} %select_maximum_fusion.2, pred[128,1024]{0,1:T(8,128)(4,1)S(1)} %broadcast_compare_fusion.2), kind=kLoop, calls=%fused_computation.7.clone.1 | loop fusion | flops 8386560 | bytes 8536064 | tf_op jit(solution)/shard_map/while/body/eval_jaxpr/reduce_sum | solution.py:92
  298.9 4.6 %fusion.75 = f32[2,8,128,128]{3,2,1,0:T(8,128)S(1)} fusion(bf16[2,1024,8,128]{3,1,0,2:T(8,128)(2,1)} %get-tuple-element.282, f32[2,8,1024,128]{3,2,1,0:T(8,128)S(1)} %copy-done.2, f32[2,8,128]{2,1,0:T(8,128)S(1)} %select_maximum_fusion.2, pred[128,1024]{0,1:T(8,128)(4,1)S(1)} %broadcast_compare_fusion.2, ...), kind=kOutput, calls=%fused_computation.16.clone.1 | convolution fusion | flops 546045952 | bytes 14827521 | tf_op jit(solution)/shard_map/while/body/eval_jaxpr/shqk,skhe->shqe/dot_general | solution.py:93
  303.6 6.2 %constant_dynamic-slice_fusion.3 = (bf16[2,1024,8,128]{3,1,0,2:T(8,128)(2,1)}, bf16[2,1024,8,128]{3,1,0,2:T(8,128)(2,1)S(1)}) fusion(bf16[2,4096,8,128]{3,1,0,2:T(8,128)(2,1)} %get-tuple-element.314, s32[]{:T(128)S(6)} %select_n.44, bf16[2,4096,8,128]{3,1,0,2:T(8,128)(2,1)} %get-tuple-element.312), kind=kLoop, calls=%fused_computation.25.clone.1 | loop fusion | bytes 16777220 | tf_op jit(solution)/shard_map/while/body/eval_jaxpr/dynamic_slice | solution.py:123
  310.0 4.6 %fusion.72 = (f32[2,8,128]{2,1,0:T(8,128)S(1)}, f32[2,8,1024,128]{3,2,1,0:T(8,128)}) fusion(pred[128,1024]{0,1:T(8,128)(4,1)S(1)} %broadcast_compare_fusion.2, bf16[2,128,8,128]{3,1,2,0:T(8,128)(2,1)S(1)} %get-tuple-element.313, bf16[2,1024,8,128]{3,1,0,2:T(8,128)(2,1)S(1)} %get-tuple-element.278), kind=kOutput, calls=%fused_computation.3.clone.1 | convolution fusion | flops 543160320 | bytes 13246464 | tf_op jit(solution)/shard_map/while/body/eval_jaxpr/sqhe,skhe->shqk/dot_general | solution.py:84
  314.6 5.2 %fusion.73 = f32[2,8,128]{2,1,0:T(8,128)S(1)} fusion(f32[2,8,1024,128]{3,2,1,0:T(8,128)} %get-tuple-element.280, f32[2,8,128]{2,1,0:T(8,128)S(1)} %select_maximum_fusion.2, pred[128,1024]{0,1:T(8,128)(4,1)S(1)} %broadcast_compare_fusion.2), kind=kLoop, calls=%fused_computation.7.clone.1 | loop fusion | flops 8386560 | bytes 8536064 | tf_op jit(solution)/shard_map/while/body/eval_jaxpr/reduce_sum | solution.py:92
  320.4 4.6 %fusion.75 = f32[2,8,128,128]{3,2,1,0:T(8,128)S(1)} fusion(bf16[2,1024,8,128]{3,1,0,2:T(8,128)(2,1)} %get-tuple-element.282, f32[2,8,1024,128]{3,2,1,0:T(8,128)S(1)} %copy-done.2, f32[2,8,128]{2,1,0:T(8,128)S(1)} %select_maximum_fusion.2, pred[128,1024]{0,1:T(8,128)(4,1)S(1)} %broadcast_compare_fusion.2, ...), kind=kOutput, calls=%fused_computation.16.clone.1 | convolution fusion | flops 546045952 | bytes 14827521 | tf_op jit(solution)/shard_map/while/body/eval_jaxpr/shqk,skhe->shqe/dot_general | solution.py:93
  327.4 62.9 %psum.7 = f32[]{:T(128)} all-reduce(f32[]{:T(128)} %convert_reduce_fusion), channel_id=1, replica_groups=mesh['seq'=32,'mp'=4] {'seq'}, use_global_device_ids=true, to_apply=%region_7.8 | all-reduce | flops 1 | bytes 8 | tf_op jit(solution)/shard_map/psum | solution.py:138
  391.0 10.2 %reduce-scatter.5.cloned.1.call-done = f32[8,4,128]{2,0,1:T(8,128)} async-done(((f32[8,128,128]{2,0,1:T(8,128)}), f32[8,4,128]{2,0,1:T(8,128)}) %reduce-scatter.5.cloned.1.call-update) | async-done | bytes 16400 | tf_op jit(solution)/shard_map/reduce_scatter | solution.py:137
  (78 shorter events, 29.5 us)
Async XLA Ops:
  6.5 12.4 %copy-start = (bf16[64,128]{1,0:T(8,128)(2,1)S(1)}, bf16[64,128]{1,0:T(8,128)(2,1)}, u32[]{:S(2)}) copy-start(bf16[64,128]{1,0:T(8,128)(2,1)} %param.11) | copy-start | bytes 49156
  6.5 3.2 copy-start.5
  6.5 82.8 %reduce-scatter.3.cloned.1.call-start = ((), (), s32[]{:S(2)}) async-start(), calls=%async_computation.2 | async-start | bytes 5242880 | tf_op jit(solution)/shard_map/reduce_scatter | solution.py:74
  14.2 13.8 %collective-permute-start = (bf16[2,128,1024]{2,1,0:T(8,128)(2,1)S(1)}, bf16[2,128,1024]{2,1,0:T(8,128)(2,1)S(1)}, u32[]{:S(2)}, u32[]{:S(2)}) collective-permute-start(bf16[2,128,1024]{2,1,0:T(8,128)(2,1)S(1)} %bitcast.106), channel_id=1, source_target_pairs={{0,4},{4,8},{8,12},{12,16},{16,20},{20,24},{24,28},{28,32},{32,36}... | collective-permute-start | bytes 1572872 | tf_op jit(solution)/shard_map/ppermute | solution.py:14
  40.7 48.6 %copy-start.4 = (bf16[3,8,128,128]{3,2,1,0:T(8,128)(2,1)S(1)}, bf16[3,8,128,128]{3,2,1,0:T(8,128)(2,1)}, u32[]{:S(2)}) copy-start(bf16[3,8,128,128]{3,2,1,0:T(8,128)(2,1)} %param.13) | copy-start | bytes 2359300
  40.7 53.7 %copy-start.6 = (s32[128]{0:T(128)S(1)}, s32[128]{0:T(128)}, u32[]{:S(2)}) copy-start(s32[128]{0:T(128)} %param.9) | copy-start | bytes 1540
  40.7 123.9 %all-gather.3.cloned.1.call-start = ((), (), s32[]{:S(2)}) async-start(), calls=%async_computation.3 | async-start | bytes 17301504 | tf_op jit(solution)/shard_map/all_gather | solution.py:114
  89.3 5.1 %copy-start.3 = (f32[2,128,1024]{2,1,0:T(8,128)S(1)}, f32[2,128,1024]{2,1,0:T(8,128)}, u32[]{:S(2)}) copy-start(f32[2,128,1024]{2,1,0:T(8,128)} %reduce-scatter.3.cloned.1.call-done) | copy-start | bytes 3145732
  91.8 147.5 %all-gather.5.cloned.1.call-start = ((), (), s32[]{:S(2)}) async-start(), calls=%async_computation.4 | async-start | bytes 17301504 | tf_op jit(solution)/shard_map/all_gather | solution.py:115
  94.1 307.1 %reduce-scatter.5.cloned.1.call-start = ((), (), s32[]{:S(2)}) async-start(), calls=%async_computation.5 | async-start | bytes 540672 | tf_op jit(solution)/shard_map/reduce_scatter | solution.py:137
  250.3 5.8 %copy-start.2 = (f32[2,8,1024,128]{3,2,1,0:T(8,128)S(1)}, f32[2,8,1024,128]{3,2,1,0:T(8,128)}, u32[]{:S(2)}) copy-start(f32[2,8,1024,128]{3,2,1,0:T(8,128)} %get-tuple-element.280) | copy-start | bytes 25165828 | tf_op jit(solution)/shard_map/while
  271.7 5.8 %copy-start.2 = (f32[2,8,1024,128]{3,2,1,0:T(8,128)S(1)}, f32[2,8,1024,128]{3,2,1,0:T(8,128)}, u32[]{:S(2)}) copy-start(f32[2,8,1024,128]{3,2,1,0:T(8,128)} %get-tuple-element.280) | copy-start | bytes 25165828 | tf_op jit(solution)/shard_map/while
  293.2 5.8 %copy-start.2 = (f32[2,8,1024,128]{3,2,1,0:T(8,128)S(1)}, f32[2,8,1024,128]{3,2,1,0:T(8,128)}, u32[]{:S(2)}) copy-start(f32[2,8,1024,128]{3,2,1,0:T(8,128)} %get-tuple-element.280) | copy-start | bytes 25165828 | tf_op jit(solution)/shard_map/while
  314.6 5.8 %copy-start.2 = (f32[2,8,1024,128]{3,2,1,0:T(8,128)S(1)}, f32[2,8,1024,128]{3,2,1,0:T(8,128)}, u32[]{:S(2)}) copy-start(f32[2,8,1024,128]{3,2,1,0:T(8,128)} %get-tuple-element.280) | copy-start | bytes 25165828 | tf_op jit(solution)/shard_map/while
  325.0 77.6 %copy-start.1 = (bf16[64,128]{1,0:T(8,128)(2,1)S(1)}, bf16[64,128]{1,0:T(8,128)(2,1)}, u32[]{:S(2)}) copy-start(bf16[64,128]{1,0:T(8,128)(2,1)} %param.11) | copy-start | bytes 49156
Sparse Core Ops, SparseCore 0:
  40.9 48.3 reduce-scatter.2
  91.9 72.7 all-gather.2
  167.2 71.9 all-gather.4
  327.0 74.2 reduce-scatter.4
where the time goes:
time: 411 us; the launch traced here: 409 us
  waiting for transfers between devices  203 us (49%)
  matrix products  65.9 us (16%)
  blocking collectives  62.9 us (15%)
  local copies, waits for them, and re-layouts  34.3 us (8%)
  other arithmetic  23.6 us (6%)
  between operations  14 us (3%)
  starting transfers between devices  4.9 us (1%)
    all_gather x1, waiting for transfers between devices, body(): lax.all_gather(value_heads, 'seq', axis=1, tiled=True)  74.6 us
    all_gather x1, waiting for transfers between devices, body(): lax.all_gather(key_heads, 'seq', axis=1, tiled=True)  69.8 us
    psum x1, blocking collectives, body(): kept_count = lax.psum(jnp.sum(pair_mask.astype(jnp.float32)), 'seq')  62.9 us
    reduce_scatter x1, waiting for transfers between devices, body(): lax.psum_scatter(partial_value, 'mp', scatter_dimension=2, tiled=True)  48.5 us
    dynamic_slice x4, local copies, waits for them, and re-layouts, advance(): lax.dynamic_slice_in_dim(member, offset, block_rows, 1)  24.7 us
    reduce_sum x4, other arithmetic, fold_block(): row_sum = row_sum * rescale + jnp.sum(weights, axis=-1)  20.8 us
    dot_general x4, matrix products, fold_block(): jnp.einsum('sqhe,skhe->shqk', queries, key_rows, preferred_element_type=j...  18.5 us
    dot_general x4, matrix products, fold_block(): jnp.einsum('shqk,skhe->shqe', weights.astype(jnp.bfloat16), value_rows, p...  18.4 us
  transfers between devices with their start and end apart: 5, of which 4 were waited for; matrix products, arithmetic and copies ran while one was open for 3% of the time, Pallas kernels for 0%

commit v1 on v0

v1 whole, which is shorter than its diff:
```python
import functools
import math

import jax
import jax.numpy as jnp
from jax import lax
from jax.experimental import pallas as pl
from jax.experimental.pallas import tpu as pltpu
from jax.sharding import PartitionSpec as P

F32 = jnp.float32
BF16 = jnp.bfloat16
MESH = pl.DeviceIdType.MESH
MASKED_SCORE = -1e30
TOK = 128
HEAD = 128
GROUP = 16
TILE = 256
CHUNK = 512


def dot(a, b):
    return jnp.dot(a, b, preferred_element_type=F32)


def dot_rows(a, b):
    return lax.dot_general(a, b, (((0,), (0,)), ((), ())), preferred_element_type=F32)


def dot_lanes(a, b):
    return lax.dot_general(a, b, (((1,), (1,)), ((), ())), preferred_element_type=F32)


def kernel(
    seq_n,
    mp_n,
    tok_ref,
    mask_ref,
    emb_hbm,
    filt_ref,
    w_hbm,
    wqkv_hbm,
    out_ref,
    emb,
    wbuf,
    wh,
    halo_tok,
    mask_all,
    frev,
    toep,
    gate_tab,
    feat0,
    win,
    hy,
    send1,
    recv1,
    send_r,
    send_l,
    recv_r,
    recv_l,
    chain_r,
    chain_l,
    own,
    mixed,
    kv,
    keys,
    vals,
    scores,
    kept,
    ex_send,
    ex_recv,
    gram_send,
    gram_recv,
    emb_sem,
    w_sem,
    wh_sem,
    halo_s,
    halo_r,
    mask_s,
    mask_r,
    s1_s,
    s1_r,
    sr_s,
    sr_r,
    sl_s,
    sl_r,
    a2a_s,
    a2a_r,
    ex_s,
    ex_r,
    gr_s,
    gr_r,
):
    me = lax.axis_index("seq")
    x = lax.axis_index("mp")
    right = lax.rem(x + 1, mp_n)
    left = lax.rem(x + mp_n - 1, mp_n)
    far = lax.rem(x + 2, mp_n)
    channels = emb.shape[2]
    pairs = 4
    my_pair = me // 8
    my_head = me // 4
    half = lax.rem(me // 2, 2)
    side = lax.rem(me, 2)
    partner = me + 1 - 2 * side
    next_seq = lax.rem(me + 1, seq_n)

    def peer(n):
        return lax.rem(me + n, seq_n)

    barrier = pltpu.get_barrier_semaphore()
    for other in (left, right):
        pl.semaphore_signal(barrier, inc=1, device_id={"mp": other}, device_id_type=MESH)

    def greet(n, carry):
        pl.semaphore_signal(barrier, inc=1, device_id={"seq": peer(n)}, device_id_type=MESH)
        return carry

    lax.fori_loop(1, seq_n, greet, 0)

    emb_copies = [
        pltpu.make_async_copy(emb_hbm.at[i], emb.at[i], emb_sem.at[i]) for i in range(3)
    ]
    for i in (1, 2, 0):
        emb_copies[i].start()
    w_copies = []
    dests = [d for _ in range(pairs) for d in (far, right, left)] + [x] * pairs
    steps = [n for n in range(pairs) for _ in range(3)] + list(range(pairs))
    for i, (d, n) in enumerate(zip(dests, steps)):
        pair = lax.rem(my_pair + n, pairs)
        col = pl.multiple_of(d * 1024 + pair * 256, 256)
        w_copies.append(
            pltpu.make_async_copy(w_hbm.at[:, pl.ds(col, 256)], wbuf.at[i], w_sem.at[i])
        )
    for copy in w_copies:
        copy.start()
    wh_copy = pltpu.make_async_copy(wqkv_hbm.at[:, my_head], wh, wh_sem)
    wh_copy.start()

    row_io = lax.broadcasted_iota(jnp.int32, (TOK, TOK), 0)
    col_io = lax.broadcasted_iota(jnp.int32, (TOK, TOK), 1)
    total_io = row_io + col_io
    reverse = jnp.where((total_io == 0) | (total_io == TOK), 1.0, 0.0).astype(BF16)
    frev[...] = dot(filt_ref[...], reverse)

    def build(g, carry):
        base = jnp.broadcast_to(frev[pl.ds(g, 1), :], (TOK, TOK))
        turned = pltpu.roll(base, 0, 1, stride=1, stride_axis=0)
        toep[g, :, 0:TOK] = jnp.where(col_io > row_io, turned, 0.0).astype(BF16)
        toep[g, :, TOK : 2 * TOK] = jnp.where(col_io <= row_io, turned, 0.0).astype(BF16)
        return carry

    lax.fori_loop(0, filt_ref.shape[0], build, 0)

    pl.semaphore_wait(barrier, seq_n + 1)

    halo = pltpu.make_async_remote_copy(
        src_ref=tok_ref,
        dst_ref=halo_tok,
        send_sem=halo_s,
        recv_sem=halo_r,
        device_id={"seq": next_seq},
        device_id_type=MESH,
    )
    halo.start()

    mask_own = pltpu.make_async_copy(mask_ref, mask_all.at[me], mask_r)
    mask_own.start()

    def send_mask(n, carry):
        pltpu.make_async_remote_copy(
            src_ref=mask_ref,
            dst_ref=mask_all.at[me],
            send_sem=mask_s,
            recv_sem=mask_r,
            device_id={"seq": peer(n)},
            device_id_type=MESH,
        ).start()
        return carry

    lax.fori_loop(1, seq_n, send_mask, 0)

    vocab = emb.shape[1]
    vocab_io = lax.broadcasted_iota(jnp.int32, (vocab, TOK), 0)

    def onehot(ids_ref):
        hot = [
            jnp.where(vocab_io == jnp.broadcast_to(ids_ref[s : s + 1, :], (vocab, TOK)), 1.0, 0.0)
            for s in range(2)
        ]
        return jnp.concatenate(hot, axis=1).astype(BF16)

    emb_copies[1].wait()
    emb_copies[2].wait()
    gate_tab[...] = (emb[1].astype(F32) * emb[2].astype(F32)).astype(BF16)
    own_hot = onehot(tok_ref)
    emb_copies[0].wait()
    feat0[...] = dot_rows(own_hot, emb[0])
    current = dot_rows(own_hot, gate_tab[...]).astype(BF16)
    lane_tiles = channels // 128
    for c in range(lane_tiles):
        for s in range(2):
            win[c, TOK : 2 * TOK, s * 128 : (s + 1) * 128] = current[
                s * TOK : (s + 1) * TOK, c * 128 : (c + 1) * 128
            ]
    halo.wait()
    before = dot_rows(onehot(halo_tok), gate_tab[...])
    before = jnp.where(me > 0, before, 0.0).astype(BF16)
    for c in range(lane_tiles):
        for s in range(2):
            win[c, 0:TOK, s * 128 : (s + 1) * 128] = before[
                s * TOK : (s + 1) * TOK, c * 128 : (c + 1) * 128
            ]

    groups = 128 // GROUP
    lane_group = lax.rem(lax.broadcasted_iota(jnp.int32, (TOK, 256), 1), 128) // GROUP

    def convolve(c, carry):
        taps = toep[pl.ds(c * groups, groups)].reshape(groups * TOK, 2 * TOK)
        every = dot(taps, win[c])
        conv = every[0:TOK]
        for g in range(1, groups):
            conv = jnp.where(lane_group == g, every[g * TOK : (g + 1) * TOK], conv)
        lanes = pl.ds(pl.multiple_of(c * 128, 128), 128)
        for s in range(2):
            rows = pl.ds(s * TOK, TOK)
            hy[rows, lanes] = (feat0[rows, lanes] * conv[:, s * 128 : (s + 1) * 128]).astype(BF16)
        return carry

    lax.fori_loop(0, lane_tiles, convolve, 0)

    def part(i):
        w_copies[i].wait()
        return dot(hy[...], wbuf[i])

    def to_side(src, dst, ssem, rsem, other):
        copy = pltpu.make_async_remote_copy(
            src_ref=src,
            dst_ref=dst,
            send_sem=ssem,
            recv_sem=rsem,
            device_id={"mp": other},
            device_id_type=MESH,
        )
        copy.start()
        return copy

    first, second = {}, {}
    for n in range(pairs):
        p_far = part(3 * n)
        for h, other in ((0, right), (1, left)):
            send1[n, h] = p_far[:, h * HEAD : (h + 1) * HEAD].astype(BF16)
            first[n, h] = to_side(
                send1.at[n, h], recv1.at[n, h], s1_s.at[n, h], s1_r.at[n, h], other
            )
        p_right = part(3 * n + 1)
        chain_r[n] = p_right[:, :HEAD]
        send_r[n, 1] = p_right[:, HEAD:].astype(BF16)
        second[n, "r", 1] = to_side(
            send_r.at[n, 1], recv_l.at[n, 1], sr_s.at[n, 1], sr_r.at[n, 1], right
        )
        p_left = part(3 * n + 2)
        chain_l[n] = p_left[:, HEAD:]
        send_l[n, 0] = p_left[:, :HEAD].astype(BF16)
        second[n, "l", 0] = to_side(
            send_l.at[n, 0], recv_r.at[n, 0], sl_s.at[n, 0], sl_r.at[n, 0], left
        )
    for n in range(pairs):
        own[n] = part(12 + n)
        first[n, 0].wait()
        send_r[n, 0] = (chain_r[n] + recv1[n, 0].astype(F32)).astype(BF16)
        second[n, "r", 0] = to_side(
            send_r.at[n, 0], recv_l.at[n, 0], sr_s.at[n, 0], sr_r.at[n, 0], right
        )
        first[n, 1].wait()
        send_l[n, 1] = (chain_l[n] + recv1[n, 1].astype(F32)).astype(BF16)
        second[n, "l", 1] = to_side(
            send_l.at[n, 1], recv_r.at[n, 1], sl_s.at[n, 1], sl_r.at[n, 1], left
        )

    def deliver(n, r):
        member = lax.rem(lax.rem(me, 8) + r, 8)
        target = lax.rem(my_pair + n, pairs) * 8 + member
        return mixed.at[n, member // 4, lax.rem(member, 2)], target

    for n in range(pairs):
        for key in (("r", 1), ("l", 0), ("r", 0), ("l", 1)):
            second[(n,) + key].wait()
        for h in range(2):
            total = own[n, :, h * HEAD : (h + 1) * HEAD]
            total = total + recv_l[n, h].astype(F32) + recv_r[n, h].astype(F32)
            total = total.astype(BF16)
            mixed[n, h, 0] = total[:TOK]
            mixed[n, h, 1] = total[TOK:]

        def send_rows(r, carry, n=n):
            src, target = deliver(n, r)
            pltpu.make_async_remote_copy(
                src_ref=src,
                dst_ref=kv.at[me],
                send_sem=a2a_s,
                recv_sem=a2a_r,
                device_id={"seq": target},
                device_id_type=MESH,
            ).start()
            return carry

        if n == 0:
            src, _ = deliver(0, 0)
            pltpu.make_async_copy(src, kv.at[me], a2a_r).start()
        lax.fori_loop(1 if n == 0 else 0, 8, send_rows, 0)

    pltpu.make_async_copy(kv, kv, a2a_r).wait()
    wh_copy.wait()

    w_kv = jnp.concatenate([wh[1], wh[2]], axis=1)
    rows_per = CHUNK // TOK

    def project(c, carry):
        rows = kv[pl.ds(c * rows_per, rows_per)].reshape(CHUNK, HEAD)
        both = dot(rows, w_kv).astype(BF16)
        keys[c] = both[:, :HEAD]
        vals[c] = both[:, HEAD:]
        return carry

    lax.fori_loop(0, seq_n * TOK // CHUNK, project, 0)

    scale = math.log2(math.e) / math.sqrt(HEAD)
    tiles = seq_n * TOK // TILE // 2

    def lane_max(s, best):
        for j in range(CHUNK // 128):
            best = jnp.maximum(best, s[:, j * 128 : (j + 1) * 128])
        return best

    ex_copies = [
        pltpu.make_async_remote_copy(
            src_ref=ex_send.at[j],
            dst_ref=ex_recv.at[j],
            send_sem=ex_s.at[j],
            recv_sem=ex_r.at[j],
            device_id={"seq": partner},
            device_id_type=MESH,
        )
        for j in range(tiles // 2)
    ]

    for n in range(tiles):
        tile = 2 * n + lax.rem(n + half, 2)
        q = dot(kv[pl.ds(2 * tile, 2)].reshape(TILE, HEAD), wh[0]).astype(BF16)

        def score(c, best):
            s = dot_lanes(q, keys[c])
            scores[c] = s
            return lane_max(s, best)

        best = jnp.full((TILE, 128), MASKED_SCORE, F32)
        if n > 0:
            best = lax.fori_loop(0, n, score, best)
        s = dot_lanes(q, keys[n])
        q_pos = tile * TILE + lax.broadcasted_iota(jnp.int32, (TILE, CHUNK), 0)
        k_pos = n * CHUNK + lax.broadcasted_iota(jnp.int32, (TILE, CHUNK), 1)
        s = jnp.where(k_pos <= q_pos, s, MASKED_SCORE)
        scores[n] = s
        top = jnp.max(lane_max(s, best), axis=1, keepdims=True)

        def weigh(c, state):
            row_sum, acc = state
            w = jnp.exp2((scores[c] - top) * scale)
            for j in range(CHUNK // 128):
                row_sum = row_sum + w[:, j * 128 : (j + 1) * 128]
            return row_sum, acc + dot(w.astype(BF16), vals[c])

        zero = jnp.zeros((TILE, HEAD), F32)
        row_sum, acc = lax.fori_loop(0, n + 1, weigh, (zero, zero))
        attended = acc / jnp.sum(row_sum, axis=1, keepdims=True)

        @pl.when(side == n % 2)
        def _(attended=attended, n=n):
            kept[n // 2] = attended

        @pl.when(side != n % 2)
        def _(attended=attended, n=n):
            ex_send[n // 2] = attended
            ex_copies[n // 2].start()

    pltpu.make_async_copy(mask_all, mask_all, mask_r).wait()
    gram = jnp.zeros((HEAD, HEAD), F32)
    for j in range(tiles // 2):
        ex_copies[j].wait()
        tile = 2 * (2 * j + side) + lax.rem(side + half, 2)
        diff = (kept[j] - ex_recv[j]).astype(BF16)
        chosen = jnp.concatenate(
            [mask_all[2 * tile].astype(F32), mask_all[2 * tile + 1].astype(F32)], axis=1
        )
        turned = (jnp.transpose(diff.astype(F32)) * chosen).astype(BF16)
        gram = gram + dot(turned, diff)

    rows_out = HEAD // seq_n
    for i in range(seq_n):
        gram_send[i] = gram[i * rows_out : (i + 1) * rows_out]
    pltpu.make_async_copy(gram_send.at[me], gram_recv.at[me], gr_r).start()

    def send_gram(n, carry):
        target = peer(n)
        pltpu.make_async_remote_copy(
            src_ref=gram_send.at[target],
            dst_ref=gram_recv.at[me],
            send_sem=gr_s,
            recv_sem=gr_r,
            device_id={"seq": target},
            device_id_type=MESH,
        ).start()
        return carry

    lax.fori_loop(1, seq_n, send_gram, 0)

    count = jnp.sum(jnp.sum(mask_all[...].astype(F32), axis=0), axis=1, keepdims=True)
    count = jnp.maximum(count, 1.0)
    pltpu.make_async_copy(gram_recv, gram_recv, gr_r).wait()
    for h in range(out_ref.shape[0]):
        total = gram_recv[4 * h] + gram_recv[4 * h + 1]
        total = total + (gram_recv[4 * h + 2] + gram_recv[4 * h + 3])
        out_ref[h] = total / count

    rest = seq_n - 1
    pltpu.make_async_copy(kv.at[pl.ds(0, rest)], kv.at[pl.ds(0, rest)], a2a_s).wait()
    pltpu.make_async_copy(mask_all.at[pl.ds(0, rest)], mask_all.at[pl.ds(0, rest)], mask_s).wait()
    pltpu.make_async_copy(gram_recv.at[pl.ds(0, rest)], gram_recv.at[pl.ds(0, rest)], gr_s).wait()


def body(seq_n, mp_n, token_ids, pair_mask, embed_table, conv_filter, w_out, w_qkv):
    vocab, _, channels = embed_table.shape
    filters = conv_filter.shape[0]
    heads = w_qkv.shape[1]
    length = seq_n * TOK
    chunks = length // CHUNK
    tiles = length // TILE // 2
    vmem = pl.BlockSpec(memory_space=pltpu.VMEM)
    hbm = pl.BlockSpec(memory_space=pl.ANY)
    dma = pltpu.SemaphoreType.DMA
    scratch = [
        pltpu.VMEM((3, vocab, channels), BF16),
        pltpu.VMEM((16, channels, 256), BF16),
        pltpu.VMEM((3, HEAD, HEAD), BF16),
        pltpu.VMEM((2, TOK), jnp.int32),
        pltpu.VMEM((seq_n, 1, TOK), jnp.int32),
        pltpu.VMEM((filters, TOK), F32),
        pltpu.VMEM((filters, TOK, 2 * TOK), BF16),
        pltpu.VMEM((vocab, channels), BF16),
        pltpu.VMEM((2 * TOK, channels), F32),
        pltpu.VMEM((channels // 128, 2 * TOK, 256), BF16),
        pltpu.VMEM((2 * TOK, channels), BF16),
        pltpu.VMEM((4, 2, 2 * TOK, HEAD), BF16),
        pltpu.VMEM((4, 2, 2 * TOK, HEAD), BF16),
        pltpu.VMEM((4, 2, 2 * TOK, HEAD), BF16),
        pltpu.VMEM((4, 2, 2 * TOK, HEAD), BF16),
        pltpu.VMEM((4, 2, 2 * TOK, HEAD), BF16),
        pltpu.VMEM((4, 2, 2 * TOK, HEAD), BF16),
        pltpu.VMEM((4, 2 * TOK, HEAD), F32),
        pltpu.VMEM((4, 2 * TOK, HEAD), F32),
        pltpu.VMEM((4, 2 * TOK, 2 * HEAD), F32),
        pltpu.VMEM((4, 2, 2, TOK, HEAD), BF16),
        pltpu.VMEM((seq_n, TOK, HEAD), BF16),
        pltpu.VMEM((chunks, CHUNK, HEAD), BF16),
        pltpu.VMEM((chunks, CHUNK, HEAD), BF16),
        pltpu.VMEM((chunks, TILE, CHUNK), F32),
        pltpu.VMEM((tiles // 2, TILE, HEAD), F32),
        pltpu.VMEM((tiles // 2, TILE, HEAD), F32),
        pltpu.VMEM((tiles // 2, TILE, HEAD), F32),
        pltpu.VMEM((seq_n, HEAD // seq_n, HEAD), F32),
        pltpu.VMEM((seq_n, HEAD // seq_n, HEAD), F32),
        dma((3,)),
        dma((16,)),
        dma,
        dma,
        dma,
        dma,
        dma,
        dma((4, 2)),
        dma((4, 2)),
        dma((4, 2)),
        dma((4, 2)),
        dma((4, 2)),
        dma((4, 2)),
        dma,
        dma,
        dma((tiles // 2,)),
        dma((tiles // 2,)),
        dma,
        dma,
    ]
    return pl.pallas_call(
        functools.partial(kernel, seq_n, mp_n),
        out_shape=jax.ShapeDtypeStruct((heads, HEAD // seq_n, HEAD), F32),
        in_specs=[vmem, vmem, hbm, vmem, hbm, hbm],
        out_specs=vmem,
        scratch_shapes=scratch,
        compiler_params=pltpu.CompilerParams(
            collective_id=0, has_side_effects=True, vmem_limit_bytes=56 * 1024 * 1024
        ),
        name="steer",
    )(
        token_ids,
        pair_mask.reshape(1, TOK),
        embed_table.transpose(1, 0, 2),
        conv_filter,
        w_out,
        w_qkv,
    )


def solution(mesh):
    in_specs = (
        P(None, "seq"),
        P("seq"),
        P(None, None, "mp"),
        P("mp", None),
        P("mp", None),
        P(None, "mp", None, None),
    )
    out_specs = P("mp", "seq", None)
    run = functools.partial(body, mesh.shape["seq"], mesh.shape["mp"])
    return jax.shard_map(run, mesh=mesh, in_specs=in_specs, out_specs=out_specs, check_vma=False)
```

time: 411 us -> 77.9 us (0.19)
  waiting for transfers between devices: 203 us -> 0 us
  Pallas kernels: 0 us -> 76.3 us
  matrix products: 65.9 us -> 0 us
  blocking collectives: 62.9 us -> 0 us
  local copies, waits for them, and re-layouts: 34.3 us -> 1.32 us
  other arithmetic: 23.6 us -> 0 us
  between operations: 14 us -> 0.01 us
  starting transfers between devices: 4.9 us -> 0 us
    all_gather x2 -> x0, waiting for transfers between devices: 144 us -> none  [the longest x1 74.6 us: body(): lax.all_gather(value_heads, 'seq', axis=1, tiled=True)]
    pallas_call x0 -> x1, Pallas kernels: none -> 76.3 us  [body(): pl.pallas_call(functools.partial(kernel, seq_n, mp_n), out_shape=jax.Shap...]
    dot_general x16 -> x0, matrix products: 65.9 us -> none  [the longest x4 18.5 us: fold_block(): jnp.einsum('sqhe,skhe->shqk', queries, key_rows, preferred_element_type=j...]
    psum x1 -> x0, blocking collectives: 62.9 us -> none  [body(): kept_count = lax.psum(jnp.sum(pair_mask.astype(jnp.float32)), 'seq')]
    reduce_scatter x2 -> x0, waiting for transfers between devices: 58.8 us -> none  [the longest x1 48.5 us: body(): lax.psum_scatter(partial_value, 'mp', scatter_dimension=2, tiled=True)]
    dynamic_slice x4 -> x0, local copies, waits for them, and re-layouts: 24.7 us -> none  [advance(): lax.dynamic_slice_in_dim(member, offset, block_rows, 1)]
    reduce_sum x5 -> x0, other arithmetic: 21.4 us -> none  [the longest x4 20.8 us: fold_block(): row_sum = row_sum * rescale + jnp.sum(weights, axis=-1)]
    ppermute x1 -> x0, starting transfers between devices: 4.59 us -> none  [from_behind(): lax.ppermute(value, axis, [(source, source + steps) for source in range(i...]
  transfers between devices with their start and end apart: 5 -> 0, of which waited for: 4 -> 0; matrix products, arithmetic and copies ran while one was open for 3% -> 0% of each run, Pallas kernels for 0% -> 0%
where the time goes in v1:
time: 77.9 us; the launch traced here: 77.6 us
  Pallas kernels  76.3 us (98%)
  local copies, waits for them, and re-layouts  1.32 us (2%)
    pallas_call x1, Pallas kernels, body(): pl.pallas_call(functools.partial(kernel, seq_n, mp_n), out_shape=jax.Shap...  76.3 us

profile of v1, /device:TPU:1, one launch (start us, length us, event | category | flops | bytes accessed | tf_op | source)
XLA Modules:
  0.0 77.6 jit_solution(17973898053177041694)
XLA Ops:
  0.0 76.3 %steer.1 = f32[8,4,128]{2,1,0:T(4,128)} custom-call(s32[2,128]{1,0:T(2,128)} %tok_ref.1, s32[1,128]{1,0:T(1,128)} %bitcast.3, bf16[3,512,1024]{2,1,0:T(8,128)(2,1)} %bitcast.2, bf16[64,128]{1,0:T(8,128)(2,1)} %filt_ref.1, bf16[1024,4096]{1,0:T(8,128)(2,1)} %w_hbm.1, bf16[3,8,128,128]{3,2,1,0:T(8,128)(2,1)} %wqkv_hbm.1), custom_call_target="tpu_custom_call" | custom-call | tf_op jit(solution)/shard_map/steer/pallas_call | solution.py:493
  76.3 1.3 %copy.8 = f32[8,4,128]{2,1,0:T(4,128)} copy(f32[8,4,128]{2,1,0:T(4,128)} %steer.1) | data formatting | bytes 32768

commit v2 on v1

--- a/solution.py
+++ b/solution.py
@@ -65,6 +65,7 @@
     kv,
     keys,
     vals,
+    queries,
     scores,
     kept,
     ex_send,
@@ -126,14 +127,15 @@
     w_copies = []
     dests = [d for _ in range(pairs) for d in (far, right, left)] + [x] * pairs
     steps = [n for n in range(pairs) for _ in range(3)] + list(range(pairs))
+    order = (0, 1, 2, 3, 12, 4, 5, 6, 13, 7, 8, 9, 14, 10, 11, 15)
     for i, (d, n) in enumerate(zip(dests, steps)):
         pair = lax.rem(my_pair + n, pairs)
         col = pl.multiple_of(d * 1024 + pair * 256, 256)
         w_copies.append(
             pltpu.make_async_copy(w_hbm.at[:, pl.ds(col, 256)], wbuf.at[i], w_sem.at[i])
         )
-    for copy in w_copies:
-        copy.start()
+    for i in order:
+        w_copies[i].start()
     wh_copy = pltpu.make_async_copy(wqkv_hbm.at[:, my_head], wh, wh_sem)
     wh_copy.start()
 
@@ -246,27 +248,30 @@
         return copy
 
     first, second = {}, {}
-    for n in range(pairs):
+
+    def send_far(n):
         p_far = part(3 * n)
         for h, other in ((0, right), (1, left)):
             send1[n, h] = p_far[:, h * HEAD : (h + 1) * HEAD].astype(BF16)
             first[n, h] = to_side(
                 send1.at[n, h], recv1.at[n, h], s1_s.at[n, h], s1_r.at[n, h], other
             )
+
+    def send_near(n):
         p_right = part(3 * n + 1)
-        chain_r[n] = p_right[:, :HEAD]
+        p_left = part(3 * n + 2)
         send_r[n, 1] = p_right[:, HEAD:].astype(BF16)
         second[n, "r", 1] = to_side(
             send_r.at[n, 1], recv_l.at[n, 1], sr_s.at[n, 1], sr_r.at[n, 1], right
         )
-        p_left = part(3 * n + 2)
-        chain_l[n] = p_left[:, HEAD:]
         send_l[n, 0] = p_left[:, :HEAD].astype(BF16)
         second[n, "l", 0] = to_side(
             send_l.at[n, 0], recv_r.at[n, 0], sl_s.at[n, 0], sl_r.at[n, 0], left
         )
-    for n in range(pairs):
-        own[n] = part(12 + n)
+        chain_r[n] = p_right[:, :HEAD]
+        chain_l[n] = p_left[:, HEAD:]
+
+    def send_chain(n):
         first[n, 0].wait()
         send_r[n, 0] = (chain_r[n] + recv1[n, 0].astype(F32)).astype(BF16)
         second[n, "r", 0] = to_side(
@@ -277,13 +282,14 @@
         second[n, "l", 1] = to_side(
             send_l.at[n, 1], recv_r.at[n, 1], sl_s.at[n, 1], sl_r.at[n, 1], left
         )
+        own[n] = part(12 + n)
 
     def deliver(n, r):
         member = lax.rem(lax.rem(me, 8) + r, 8)
         target = lax.rem(my_pair + n, pairs) * 8 + member
         return mixed.at[n, member // 4, lax.rem(member, 2)], target
 
-    for n in range(pairs):
+    def spread(n):
         for key in (("r", 1), ("l", 0), ("r", 0), ("l", 1)):
             second[(n,) + key].wait()
         for h in range(2):
@@ -310,17 +316,30 @@
             pltpu.make_async_copy(src, kv.at[me], a2a_r).start()
         lax.fori_loop(1 if n == 0 else 0, 8, send_rows, 0)
 
+    send_far(0)
+    send_near(0)
+    send_far(1)
+    for n in range(pairs):
+        send_chain(n)
+        if n + 1 < pairs:
+            send_near(n + 1)
+        if n + 2 < pairs:
+            send_far(n + 2)
+        if n > 0:
+            spread(n - 1)
+    spread(pairs - 1)
+
     pltpu.make_async_copy(kv, kv, a2a_r).wait()
     wh_copy.wait()
 
-    w_kv = jnp.concatenate([wh[1], wh[2]], axis=1)
     rows_per = CHUNK // TOK
 
     def project(c, carry):
         rows = kv[pl.ds(c * rows_per, rows_per)].reshape(CHUNK, HEAD)
-        both = dot(rows, w_kv).astype(BF16)
-        keys[c] = both[:, :HEAD]
-        vals[c] = both[:, HEAD:]
+        keys[c] = dot(rows, wh[1]).astype(BF16)
+        vals[c] = lax.dot_general(
+            wh[2], rows, (((0,), (1,)), ((), ())), preferred_element_type=F32
+        ).astype(BF16)
         return carry
 
     lax.fori_loop(0, seq_n * TOK // CHUNK, project, 0)
@@ -328,10 +347,15 @@
     scale = math.log2(math.e) / math.sqrt(HEAD)
     tiles = seq_n * TOK // TILE // 2
 
-    def lane_max(s, best):
-        for j in range(CHUNK // 128):
-            best = jnp.maximum(best, s[:, j * 128 : (j + 1) * 128])
-        return best
+    def tile_of(n):
+        return 2 * n + lax.rem(n + half, 2)
+
+    for n in range(tiles):
+        rows = kv[pl.ds(2 * tile_of(n), 2)].reshape(TILE, HEAD)
+        queries[n] = dot(rows, wh[0]).astype(BF16)
+
+    def fold(s):
+        return s.reshape(CHUNK // 8, 8, TILE)
 
     ex_copies = [
         pltpu.make_async_remote_copy(
@@ -345,35 +369,28 @@
         for j in range(tiles // 2)
     ]
 
+    low = jnp.full((8, TILE), MASKED_SCORE, F32)
+    best = low
     for n in range(tiles):
-        tile = 2 * n + lax.rem(n + half, 2)
-        q = dot(kv[pl.ds(2 * tile, 2)].reshape(TILE, HEAD), wh[0]).astype(BF16)
-
-        def score(c, best):
-            s = dot_lanes(q, keys[c])
-            scores[c] = s
-            return lane_max(s, best)
-
-        best = jnp.full((TILE, 128), MASKED_SCORE, F32)
-        if n > 0:
-            best = lax.fori_loop(0, n, score, best)
-        s = dot_lanes(q, keys[n])
-        q_pos = tile * TILE + lax.broadcasted_iota(jnp.int32, (TILE, CHUNK), 0)
-        k_pos = n * CHUNK + lax.broadcasted_iota(jnp.int32, (TILE, CHUNK), 1)
+        s = dot_lanes(keys[n], queries[n])
+        q_pos = tile_of(n) * TILE + lax.broadcasted_iota(jnp.int32, (CHUNK, TILE), 1)
+        k_pos = n * CHUNK + lax.broadcasted_iota(jnp.int32, (CHUNK, TILE), 0)
         s = jnp.where(k_pos <= q_pos, s, MASKED_SCORE)
-        scores[n] = s
-        top = jnp.max(lane_max(s, best), axis=1, keepdims=True)
-
-        def weigh(c, state):
-            row_sum, acc = state
-            w = jnp.exp2((scores[c] - top) * scale)
-            for j in range(CHUNK // 128):
-                row_sum = row_sum + w[:, j * 128 : (j + 1) * 128]
-            return row_sum, acc + dot(w.astype(BF16), vals[c])
-
-        zero = jnp.zeros((TILE, HEAD), F32)
-        row_sum, acc = lax.fori_loop(0, n + 1, weigh, (zero, zero))
-        attended = acc / jnp.sum(row_sum, axis=1, keepdims=True)
+        scores[n % 2, n] = s
+        best = jnp.maximum(best, jnp.max(fold(s), axis=0))
+        top = jnp.max(best, axis=0, keepdims=True)
+        best = low
+        row_sum = jnp.zeros((8, TILE), F32)
+        acc = jnp.zeros((HEAD, TILE), F32)
+        for c in range(n + 1):
+            w = jnp.exp2((scores[n % 2, c] - top) * scale)
+            row_sum = row_sum + jnp.sum(fold(w), axis=0)
+            acc = acc + dot(vals[c], w.astype(BF16))
+            if n + 1 < tiles:
+                s = dot_lanes(keys[c], queries[n + 1])
+                scores[(n + 1) % 2, c] = s
+                best = jnp.maximum(best, jnp.max(fold(s), axis=0))
+        attended = acc / jnp.sum(row_sum, axis=0, keepdims=True)
 
         @pl.when(side == n % 2)
         def _(attended=attended, n=n):
@@ -393,8 +410,7 @@
         chosen = jnp.concatenate(
             [mask_all[2 * tile].astype(F32), mask_all[2 * tile + 1].astype(F32)], axis=1
         )
-        turned = (jnp.transpose(diff.astype(F32)) * chosen).astype(BF16)
-        gram = gram + dot(turned, diff)
+        gram = gram + dot_lanes((diff.astype(F32) * chosen).astype(BF16), diff)
 
     rows_out = HEAD // seq_n
     for i in range(seq_n):
@@ -463,11 +479,12 @@
         pltpu.VMEM((4, 2, 2, TOK, HEAD), BF16),
         pltpu.VMEM((seq_n, TOK, HEAD), BF16),
         pltpu.VMEM((chunks, CHUNK, HEAD), BF16),
-        pltpu.VMEM((chunks, CHUNK, HEAD), BF16),
-        pltpu.VMEM((chunks, TILE, CHUNK), F32),
-        pltpu.VMEM((tiles // 2, TILE, HEAD), F32),
-        pltpu.VMEM((tiles // 2, TILE, HEAD), F32),
-        pltpu.VMEM((tiles // 2, TILE, HEAD), F32),
+        pltpu.VMEM((chunks, HEAD, CHUNK), BF16),
+        pltpu.VMEM((tiles, TILE, HEAD), BF16),
+        pltpu.VMEM((2, chunks, CHUNK, TILE), F32),
+        pltpu.VMEM((tiles // 2, HEAD, TILE), F32),
+        pltpu.VMEM((tiles // 2, HEAD, TILE), F32),
+        pltpu.VMEM((tiles // 2, HEAD, TILE), F32),
         pltpu.VMEM((seq_n, HEAD // seq_n, HEAD), F32),
         pltpu.VMEM((seq_n, HEAD // seq_n, HEAD), F32),
         dma((3,)),

time: 77.9 us -> 65.1 us (0.84)
  Pallas kernels: 76.3 us -> 63.5 us
    pallas_call x1, Pallas kernels: 76.3 us -> 63.5 us  [body(): pl.pallas_call(functools.partial(kernel, seq_n, mp_n), out_shape=jax.Shap...]
where the time goes in v2:
time: 65.1 us; the launch traced here: 64.9 us
  Pallas kernels  63.5 us (98%)
  local copies, waits for them, and re-layouts  1.32 us (2%)
    pallas_call x1, Pallas kernels, body(): pl.pallas_call(functools.partial(kernel, seq_n, mp_n), out_shape=jax.Shap...  63.5 us
    unnamed x1, local copies, waits for them, and re-layouts  1.32 us

profile of v2, /device:TPU:1, one launch (start us, length us, event | category | flops | bytes accessed | tf_op | source)
XLA Modules:
  0.0 64.9 jit_solution(10028565073155330499)
XLA Ops:
  0.0 63.5 %steer.1 = f32[8,4,128]{2,1,0:T(4,128)} custom-call(s32[2,128]{1,0:T(2,128)} %tok_ref.1, s32[1,128]{1,0:T(1,128)} %bitcast.3, bf16[3,512,1024]{2,1,0:T(8,128)(2,1)} %bitcast.2, bf16[64,128]{1,0:T(8,128)(2,1)} %filt_ref.1, bf16[1024,4096]{1,0:T(8,128)(2,1)} %w_hbm.1, bf16[3,8,128,128]{3,2,1,0:T(8,128)(2,1)} %wqkv_hbm.1), custom_call_target="tpu_custom_call" | custom-call | tf_op jit(solution)/shard_map/steer/pallas_call | solution.py:510
  63.5 1.3 %copy.8 = f32[8,4,128]{2,1,0:T(4,128)} copy(f32[8,4,128]{2,1,0:T(4,128)} %steer.1) | data formatting | bytes 32768

commit v3 on v2

--- a/solution.py
+++ b/solution.py
@@ -17,6 +17,7 @@
 GROUP = 16
 TILE = 256
 CHUNK = 512
+OFFSETS = (2, 1, 3, 0)
 
 
 def dot(a, b):
@@ -67,8 +68,7 @@
     vals,
     queries,
     scores,
-    kept,
-    ex_send,
+    attended,
     ex_recv,
     gram_send,
     gram_recv,
@@ -87,6 +87,8 @@
     sl_r,
     a2a_s,
     a2a_r,
+    fwd_s,
+    fwd_r,
     ex_s,
     ex_r,
     gr_s,
@@ -127,9 +129,9 @@
     w_copies = []
     dests = [d for _ in range(pairs) for d in (far, right, left)] + [x] * pairs
     steps = [n for n in range(pairs) for _ in range(3)] + list(range(pairs))
-    order = (0, 1, 2, 3, 12, 4, 5, 6, 13, 7, 8, 9, 14, 10, 11, 15)
+    order = (0, 3, 6, 9, 1, 2, 12, 4, 5, 13, 7, 8, 14, 10, 11, 15)
     for i, (d, n) in enumerate(zip(dests, steps)):
-        pair = lax.rem(my_pair + n, pairs)
+        pair = lax.rem(my_pair + OFFSETS[n], pairs)
         col = pl.multiple_of(d * 1024 + pair * 256, 256)
         w_copies.append(
             pltpu.make_async_copy(w_hbm.at[:, pl.ds(col, 256)], wbuf.at[i], w_sem.at[i])
@@ -144,43 +146,6 @@
     total_io = row_io + col_io
     reverse = jnp.where((total_io == 0) | (total_io == TOK), 1.0, 0.0).astype(BF16)
     frev[...] = dot(filt_ref[...], reverse)
-
-    def build(g, carry):
-        base = jnp.broadcast_to(frev[pl.ds(g, 1), :], (TOK, TOK))
-        turned = pltpu.roll(base, 0, 1, stride=1, stride_axis=0)
-        toep[g, :, 0:TOK] = jnp.where(col_io > row_io, turned, 0.0).astype(BF16)
-        toep[g, :, TOK : 2 * TOK] = jnp.where(col_io <= row_io, turned, 0.0).astype(BF16)
-        return carry
-
-    lax.fori_loop(0, filt_ref.shape[0], build, 0)
-
-    pl.semaphore_wait(barrier, seq_n + 1)
-
-    halo = pltpu.make_async_remote_copy(
-        src_ref=tok_ref,
-        dst_ref=halo_tok,
-        send_sem=halo_s,
-        recv_sem=halo_r,
-        device_id={"seq": next_seq},
-        device_id_type=MESH,
-    )
-    halo.start()
-
-    mask_own = pltpu.make_async_copy(mask_ref, mask_all.at[me], mask_r)
-    mask_own.start()
-
-    def send_mask(n, carry):
-        pltpu.make_async_remote_copy(
-            src_ref=mask_ref,
-            dst_ref=mask_all.at[me],
-            send_sem=mask_s,
-            recv_sem=mask_r,
-            device_id={"seq": peer(n)},
-            device_id_type=MESH,
-        ).start()
-        return carry
-
-    lax.fori_loop(1, seq_n, send_mask, 0)
 
     vocab = emb.shape[1]
     vocab_io = lax.broadcasted_iota(jnp.int32, (vocab, TOK), 0)
@@ -205,6 +170,43 @@
             win[c, TOK : 2 * TOK, s * 128 : (s + 1) * 128] = current[
                 s * TOK : (s + 1) * TOK, c * 128 : (c + 1) * 128
             ]
+    pl.semaphore_wait(barrier, seq_n + 1)
+
+    halo = pltpu.make_async_remote_copy(
+        src_ref=tok_ref,
+        dst_ref=halo_tok,
+        send_sem=halo_s,
+        recv_sem=halo_r,
+        device_id={"seq": next_seq},
+        device_id_type=MESH,
+    )
+    halo.start()
+
+    mask_own = pltpu.make_async_copy(mask_ref, mask_all.at[me], mask_r)
+    mask_own.start()
+
+    def send_mask(n, carry):
+        pltpu.make_async_remote_copy(
+            src_ref=mask_ref,
+            dst_ref=mask_all.at[me],
+            send_sem=mask_s,
+            recv_sem=mask_r,
+            device_id={"seq": peer(n)},
+            device_id_type=MESH,
+        ).start()
+        return carry
+
+    lax.fori_loop(1, seq_n, send_mask, 0)
+
+    def build(g, carry):
+        base = jnp.broadcast_to(frev[pl.ds(g, 1), :], (TOK, TOK))
+        turned = pltpu.roll(base, 0, 1, stride=1, stride_axis=0)
+        toep[g, :, 0:TOK] = jnp.where(col_io > row_io, turned, 0.0).astype(BF16)
+        toep[g, :, TOK : 2 * TOK] = jnp.where(col_io <= row_io, turned, 0.0).astype(BF16)
+        return carry
+
+    lax.fori_loop(0, filt_ref.shape[0], build, 0)
+
     halo.wait()
     before = dot_rows(onehot(halo_tok), gate_tab[...])
     before = jnp.where(me > 0, before, 0.0).astype(BF16)
@@ -217,19 +219,16 @@
     groups = 128 // GROUP
     lane_group = lax.rem(lax.broadcasted_iota(jnp.int32, (TOK, 256), 1), 128) // GROUP
 
-    def convolve(c, carry):
-        taps = toep[pl.ds(c * groups, groups)].reshape(groups * TOK, 2 * TOK)
+    for c in range(lane_tiles):
+        taps = toep[c * groups : (c + 1) * groups].reshape(groups * TOK, 2 * TOK)
         every = dot(taps, win[c])
         conv = every[0:TOK]
         for g in range(1, groups):
             conv = jnp.where(lane_group == g, every[g * TOK : (g + 1) * TOK], conv)
-        lanes = pl.ds(pl.multiple_of(c * 128, 128), 128)
+        lanes = pl.ds(c * 128, 128)
         for s in range(2):
             rows = pl.ds(s * TOK, TOK)
             hy[rows, lanes] = (feat0[rows, lanes] * conv[:, s * 128 : (s + 1) * 128]).astype(BF16)
-        return carry
-
-    lax.fori_loop(0, lane_tiles, convolve, 0)
 
     def part(i):
         w_copies[i].wait()
@@ -249,100 +248,156 @@
 
     first, second = {}, {}
 
-    def send_far(n):
-        p_far = part(3 * n)
+    def rows_of(s):
+        return pl.ds(s * TOK, TOK)
+
+    def send_far(n, s):
+        if s == 0:
+            p_far = part(3 * n)
+            for h in range(2):
+                send1[n, h] = p_far[:, h * HEAD : (h + 1) * HEAD].astype(BF16)
         for h, other in ((0, right), (1, left)):
-            send1[n, h] = p_far[:, h * HEAD : (h + 1) * HEAD].astype(BF16)
-            first[n, h] = to_side(
-                send1.at[n, h], recv1.at[n, h], s1_s.at[n, h], s1_r.at[n, h], other
+            first[n, h, s] = to_side(
+                send1.at[n, h, rows_of(s)],
+                recv1.at[n, h, rows_of(s)],
+                s1_s.at[n, h, s],
+                s1_r.at[n, h, s],
+                other,
             )
 
-    def send_near(n):
-        p_right = part(3 * n + 1)
-        p_left = part(3 * n + 2)
-        send_r[n, 1] = p_right[:, HEAD:].astype(BF16)
-        second[n, "r", 1] = to_side(
-            send_r.at[n, 1], recv_l.at[n, 1], sr_s.at[n, 1], sr_r.at[n, 1], right
+    def send_right(n, h, s):
+        second[n, "r", h, s] = to_side(
+            send_r.at[n, h, rows_of(s)],
+            recv_l.at[n, h, rows_of(s)],
+            sr_s.at[n, h, s],
+            sr_r.at[n, h, s],
+            right,
         )
-        send_l[n, 0] = p_left[:, :HEAD].astype(BF16)
-        second[n, "l", 0] = to_side(
-            send_l.at[n, 0], recv_r.at[n, 0], sl_s.at[n, 0], sl_r.at[n, 0], left
+
+    def send_left(n, h, s):
+        second[n, "l", h, s] = to_side(
+            send_l.at[n, h, rows_of(s)],
+            recv_r.at[n, h, rows_of(s)],
+            sl_s.at[n, h, s],
+            sl_r.at[n, h, s],
+            left,
         )
-        chain_r[n] = p_right[:, :HEAD]
-        chain_l[n] = p_left[:, HEAD:]
-
-    def send_chain(n):
-        first[n, 0].wait()
-        send_r[n, 0] = (chain_r[n] + recv1[n, 0].astype(F32)).astype(BF16)
-        second[n, "r", 0] = to_side(
-            send_r.at[n, 0], recv_l.at[n, 0], sr_s.at[n, 0], sr_r.at[n, 0], right
-        )
-        first[n, 1].wait()
-        send_l[n, 1] = (chain_l[n] + recv1[n, 1].astype(F32)).astype(BF16)
-        second[n, "l", 1] = to_side(
-            send_l.at[n, 1], recv_r.at[n, 1], sl_s.at[n, 1], sl_r.at[n, 1], left
-        )
-        own[n] = part(12 + n)
-
-    def deliver(n, r):
-        member = lax.rem(lax.rem(me, 8) + r, 8)
-        target = lax.rem(my_pair + n, pairs) * 8 + member
-        return mixed.at[n, member // 4, lax.rem(member, 2)], target
-
-    def spread(n):
+
+    def send_near(n, s):
+        if s == 0:
+            p_right = part(3 * n + 1)
+            send_r[n, 1] = p_right[:, HEAD:].astype(BF16)
+            chain_r[n] = p_right[:, :HEAD]
+            p_left = part(3 * n + 2)
+            send_l[n, 0] = p_left[:, :HEAD].astype(BF16)
+            chain_l[n] = p_left[:, HEAD:]
+        send_right(n, 1, s)
+        send_left(n, 0, s)
+
+    def send_chain(n, s):
+        rows = rows_of(s)
+        first[n, 0, s].wait()
+        send_r[n, 0, rows] = (chain_r[n, rows] + recv1[n, 0, rows].astype(F32)).astype(BF16)
+        send_right(n, 0, s)
+        first[n, 1, s].wait()
+        send_l[n, 1, rows] = (chain_l[n, rows] + recv1[n, 1, rows].astype(F32)).astype(BF16)
+        send_left(n, 1, s)
+        if s == 0:
+            own[n] = part(12 + n)
+
+    my_y = lax.rem(me // 2, 4)
+    other_chip = me + 2 - 4 * half
+
+    def send_rows(n, h, s, target, sem):
+        pltpu.make_async_remote_copy(
+            src_ref=mixed.at[n, h, s],
+            dst_ref=kv.at[me],
+            send_sem=a2a_s,
+            recv_sem=sem,
+            device_id={"seq": target},
+            device_id_type=MESH,
+        ).start()
+
+    def spread(n, s):
+        rows = rows_of(s)
         for key in (("r", 1), ("l", 0), ("r", 0), ("l", 1)):
-            second[(n,) + key].wait()
+            second[(n,) + key + (s,)].wait()
         for h in range(2):
-            total = own[n, :, h * HEAD : (h + 1) * HEAD]
-            total = total + recv_l[n, h].astype(F32) + recv_r[n, h].astype(F32)
-            total = total.astype(BF16)
-            mixed[n, h, 0] = total[:TOK]
-            mixed[n, h, 1] = total[TOK:]
-
-        def send_rows(r, carry, n=n):
-            src, target = deliver(n, r)
-            pltpu.make_async_remote_copy(
-                src_ref=src,
-                dst_ref=kv.at[me],
-                send_sem=a2a_s,
-                recv_sem=a2a_r,
-                device_id={"seq": target},
+            total = own[n, rows, h * HEAD : (h + 1) * HEAD]
+            total = total + recv_l[n, h, rows].astype(F32) + recv_r[n, h, rows].astype(F32)
+            mixed[n, h, s] = total.astype(BF16)
+        base = lax.rem(my_pair + OFFSETS[n], pairs) * 8 + s
+        for h in range(2):
+            if False:
+                near_y = jnp.where(my_y // 2 == h, my_y, 3 - my_y)
+                send_rows(n, h, s, base + 2 * near_y, a2a_r.at[n])
+            else:
+                for a in range(2):
+                    target = base + 2 * (2 * h + a)
+
+                    if OFFSETS[n] > 0:
+                        send_rows(n, h, s, target, a2a_r.at[n])
+                        continue
+
+                    @pl.when(target == me)
+                    def _(h=h):
+                        pltpu.make_async_copy(mixed.at[n, h, s], kv.at[me], a2a_r.at[n]).start()
+
+                    @pl.when(target != me)
+                    def _(h=h, target=target):
+                        send_rows(n, h, s, target, a2a_r.at[n])
+
+    def origin(n):
+        return lax.rem(my_pair - OFFSETS[n] + pairs, pairs)
+
+    def arrived(n, blocks, sem):
+        part_of = kv.at[pl.ds(origin(n) * 8, blocks)]
+        pltpu.make_async_copy(part_of, part_of, sem).wait()
+
+    forwards = []
+
+    def forward(n):
+        arrived(n, 4, a2a_r.at[n])
+        for i, y in enumerate((my_y, 3 - my_y)):
+            blocks = kv.at[pl.ds(origin(n) * 8 + 2 * y, 2)]
+            copy = pltpu.make_async_remote_copy(
+                src_ref=blocks,
+                dst_ref=blocks,
+                send_sem=fwd_s.at[n, i],
+                recv_sem=fwd_r.at[n, i],
+                device_id={"seq": other_chip},
                 device_id_type=MESH,
-            ).start()
-            return carry
-
-        if n == 0:
-            src, _ = deliver(0, 0)
-            pltpu.make_async_copy(src, kv.at[me], a2a_r).start()
-        lax.fori_loop(1 if n == 0 else 0, 8, send_rows, 0)
-
-    send_far(0)
-    send_near(0)
-    send_far(1)
+            )
+            copy.start()
+            forwards.append(copy)
+
+    rows_per = CHUNK // TOK
+
+    def project(n):
+        arrived(n, 8, a2a_r.at[n])
+        for i in range(2):
+            c = origin(n) * 2 + i
+            rows = kv[pl.ds(c * rows_per, rows_per)].reshape(CHUNK, HEAD)
+            keys[c] = dot(rows, wh[1]).astype(BF16)
+            vals[c] = lax.dot_general(
+                wh[2], rows, (((0,), (1,)), ((), ())), preferred_element_type=F32
+            ).astype(BF16)
+
+    halves = [(n, s) for n in range(pairs) for s in range(2)]
+    for n, s in halves:
+        send_far(n, s)
+    ahead = 3
+    for n, s in halves[:ahead]:
+        send_near(n, s)
+        send_chain(n, s)
+    for i, (n, s) in enumerate(halves):
+        spread(n, s)
+        if i + ahead < len(halves):
+            send_near(*halves[i + ahead])
+            send_chain(*halves[i + ahead])
+    wh_copy.wait()
     for n in range(pairs):
-        send_chain(n)
-        if n + 1 < pairs:
-            send_near(n + 1)
-        if n + 2 < pairs:
-            send_far(n + 2)
-        if n > 0:
-            spread(n - 1)
-    spread(pairs - 1)
-
-    pltpu.make_async_copy(kv, kv, a2a_r).wait()
-    wh_copy.wait()
-
-    rows_per = CHUNK // TOK
-
-    def project(c, carry):
-        rows = kv[pl.ds(c * rows_per, rows_per)].reshape(CHUNK, HEAD)
-        keys[c] = dot(rows, wh[1]).astype(BF16)
-        vals[c] = lax.dot_general(
-            wh[2], rows, (((0,), (1,)), ((), ())), preferred_element_type=F32
-        ).astype(BF16)
-        return carry
-
-    lax.fori_loop(0, seq_n * TOK // CHUNK, project, 0)
+        project(n)
 
     scale = math.log2(math.e) / math.sqrt(HEAD)
     tiles = seq_n * TOK // TILE // 2
@@ -359,7 +414,7 @@
 
     ex_copies = [
         pltpu.make_async_remote_copy(
-            src_ref=ex_send.at[j],
+            src_ref=attended.at[2 * j + 1 - side],
             dst_ref=ex_recv.at[j],
             send_sem=ex_s.at[j],
             recv_sem=ex_r.at[j],
@@ -369,6 +424,17 @@
         for j in range(tiles // 2)
     ]
 
+    def finish(j, gram):
+        ex_copies[j].wait()
+        tile = tile_of(2 * j + side)
+        diff = (attended[2 * j + side] - ex_recv[j]).astype(BF16)
+        chosen = jnp.concatenate(
+            [mask_all[2 * tile].astype(F32), mask_all[2 * tile + 1].astype(F32)], axis=1
+        )
+        return gram + dot_lanes((diff.astype(F32) * chosen).astype(BF16), diff)
+
+    pltpu.make_async_copy(mask_all, mask_all, mask_r).wait()
+    gram = jnp.zeros((HEAD, HEAD), F32)
     low = jnp.full((8, TILE), MASKED_SCORE, F32)
     best = low
     for n in range(tiles):
@@ -390,27 +456,12 @@
                 s = dot_lanes(keys[c], queries[n + 1])
                 scores[(n + 1) % 2, c] = s
                 best = jnp.maximum(best, jnp.max(fold(s), axis=0))
-        attended = acc / jnp.sum(row_sum, axis=0, keepdims=True)
-
-        @pl.when(side == n % 2)
-        def _(attended=attended, n=n):
-            kept[n // 2] = attended
-
-        @pl.when(side != n % 2)
-        def _(attended=attended, n=n):
-            ex_send[n // 2] = attended
+        attended[n] = acc / jnp.sum(row_sum, axis=0, keepdims=True)
+        if n % 2 == 1:
             ex_copies[n // 2].start()
-
-    pltpu.make_async_copy(mask_all, mask_all, mask_r).wait()
-    gram = jnp.zeros((HEAD, HEAD), F32)
-    for j in range(tiles // 2):
-        ex_copies[j].wait()
-        tile = 2 * (2 * j + side) + lax.rem(side + half, 2)
-        diff = (kept[j] - ex_recv[j]).astype(BF16)
-        chosen = jnp.concatenate(
-            [mask_all[2 * tile].astype(F32), mask_all[2 * tile + 1].astype(F32)], axis=1
-        )
-        gram = gram + dot_lanes((diff.astype(F32) * chosen).astype(BF16), diff)
+        elif n > 0:
+            gram = finish(n // 2 - 1, gram)
+    gram = finish(tiles // 2 - 1, gram)
 
     rows_out = HEAD // seq_n
     for i in range(seq_n):
@@ -440,7 +491,8 @@
         out_ref[h] = total / count
 
     rest = seq_n - 1
-    pltpu.make_async_copy(kv.at[pl.ds(0, rest)], kv.at[pl.ds(0, rest)], a2a_s).wait()
+    direct = kv.at[pl.ds(0, 31)]
+    pltpu.make_async_copy(direct, direct, a2a_s).wait()
     pltpu.make_async_copy(mask_all.at[pl.ds(0, rest)], mask_all.at[pl.ds(0, rest)], mask_s).wait()
     pltpu.make_async_copy(gram_recv.at[pl.ds(0, rest)], gram_recv.at[pl.ds(0, rest)], gr_s).wait()
 
@@ -482,8 +534,7 @@
         pltpu.VMEM((chunks, HEAD, CHUNK), BF16),
         pltpu.VMEM((tiles, TILE, HEAD), BF16),
         pltpu.VMEM((2, chunks, CHUNK, TILE), F32),
-        pltpu.VMEM((tiles // 2, HEAD, TILE), F32),
-        pltpu.VMEM((tiles // 2, HEAD, TILE), F32),
+        pltpu.VMEM((tiles, HEAD, TILE), F32),
         pltpu.VMEM((tiles // 2, HEAD, TILE), F32),
         pltpu.VMEM((seq_n, HEAD // seq_n, HEAD), F32),
         pltpu.VMEM((seq_n, HEAD // seq_n, HEAD), F32),
@@ -494,14 +545,16 @@
         dma,
         dma,
         dma,
-        dma((4, 2)),
-        dma((4, 2)),
-        dma((4, 2)),
-        dma((4, 2)),
-        dma((4, 2)),
-        dma((4, 2)),
-        dma,
-        dma,
+        dma((4, 2, 2)),
+        dma((4, 2, 2)),
+        dma((4, 2, 2)),
+        dma((4, 2, 2)),
+        dma((4, 2, 2)),
+        dma((4, 2, 2)),
+        dma,
+        dma((4,)),
+        dma((3, 2)),
+        dma((3, 2)),
         dma((tiles // 2,)),
         dma((tiles // 2,)),
         dma,

time: 65.1 us -> 61.4 us (0.943)
  Pallas kernels: 63.5 us -> 59.8 us
    pallas_call x1, Pallas kernels: 63.5 us -> 59.8 us  [body(): pl.pallas_call(functools.partial(kernel, seq_n, mp_n), out_shape=jax.Shap...]
where the time goes in v3:
time: 61.4 us; the launch traced here: 61.2 us
  Pallas kernels  59.8 us (97%)
  local copies, waits for them, and re-layouts  1.32 us (2%)
    pallas_call x1, Pallas kernels, body(): pl.pallas_call(functools.partial(kernel, seq_n, mp_n), out_shape=jax.Shap...  59.8 us
    unnamed x1, local copies, waits for them, and re-layouts  1.32 us

profile of v3, /device:TPU:1, one launch (start us, length us, event | category | flops | bytes accessed | tf_op | source)
XLA Modules:
  0.0 61.2 jit_solution(13569967749128001141)
XLA Ops:
  0.0 59.8 %steer.1 = f32[8,4,128]{2,1,0:T(4,128)} custom-call(s32[2,128]{1,0:T(2,128)} %tok_ref.1, s32[1,128]{1,0:T(1,128)} %bitcast.3, bf16[3,512,1024]{2,1,0:T(8,128)(2,1)} %bitcast.2, bf16[64,128]{1,0:T(8,128)(2,1)} %filt_ref.1, bf16[1024,4096]{1,0:T(8,128)(2,1)} %w_hbm.1, bf16[3,8,128,128]{3,2,1,0:T(8,128)(2,1)} %wqkv_hbm.1), custom_call_target="tpu_custom_call" | custom-call | tf_op jit(solution)/shard_map/steer/pallas_call | solution.py:563
  59.8 1.3 %copy.8 = f32[8,4,128]{2,1,0:T(4,128)} copy(f32[8,4,128]{2,1,0:T(4,128)} %steer.1) | data formatting | bytes 32768

commit v4 on v3

--- a/solution.py
+++ b/solution.py
@@ -136,8 +136,6 @@
         w_copies.append(
             pltpu.make_async_copy(w_hbm.at[:, pl.ds(col, 256)], wbuf.at[i], w_sem.at[i])
         )
-    for i in order:
-        w_copies[i].start()
     wh_copy = pltpu.make_async_copy(wqkv_hbm.at[:, my_head], wh, wh_sem)
     wh_copy.start()
 
@@ -148,22 +146,24 @@
     frev[...] = dot(filt_ref[...], reverse)
 
     vocab = emb.shape[1]
-    vocab_io = lax.broadcasted_iota(jnp.int32, (vocab, TOK), 0)
+    vocab_io = lax.broadcasted_iota(jnp.int32, (TOK, TOK), 1).astype(F32)
 
     def onehot(ids_ref):
-        hot = [
-            jnp.where(vocab_io == jnp.broadcast_to(ids_ref[s : s + 1, :], (vocab, TOK)), 1.0, 0.0)
-            for s in range(2)
-        ]
-        return jnp.concatenate(hot, axis=1).astype(BF16)
+        rows = []
+        for s in range(2):
+            ids = jnp.broadcast_to(ids_ref[s : s + 1, :].astype(F32), (TOK, TOK))
+            ids = jnp.transpose(ids)
+            hot = [jnp.where(ids == vocab_io + v, 1.0, 0.0) for v in range(0, vocab, TOK)]
+            rows.append(jnp.concatenate(hot, axis=1))
+        return jnp.concatenate(rows, axis=0).astype(BF16)
 
     emb_copies[1].wait()
     emb_copies[2].wait()
     gate_tab[...] = (emb[1].astype(F32) * emb[2].astype(F32)).astype(BF16)
     own_hot = onehot(tok_ref)
     emb_copies[0].wait()
-    feat0[...] = dot_rows(own_hot, emb[0])
-    current = dot_rows(own_hot, gate_tab[...]).astype(BF16)
+    feat0[...] = dot(own_hot, emb[0])
+    current = dot(own_hot, gate_tab[...]).astype(BF16)
     lane_tiles = channels // 128
     for c in range(lane_tiles):
         for s in range(2):
@@ -181,34 +181,24 @@
         device_id_type=MESH,
     )
     halo.start()
-
-    mask_own = pltpu.make_async_copy(mask_ref, mask_all.at[me], mask_r)
-    mask_own.start()
-
-    def send_mask(n, carry):
-        pltpu.make_async_remote_copy(
-            src_ref=mask_ref,
-            dst_ref=mask_all.at[me],
-            send_sem=mask_s,
-            recv_sem=mask_r,
-            device_id={"seq": peer(n)},
-            device_id_type=MESH,
-        ).start()
+    for i in order:
+        w_copies[i].start()
+
+    unroll = 8
+
+    def build(step, carry):
+        for i in range(unroll):
+            g = step * unroll + i
+            base = jnp.broadcast_to(frev[pl.ds(g, 1), :], (TOK, TOK))
+            turned = pltpu.roll(base, 0, 1, stride=1, stride_axis=0)
+            toep[g, :, 0:TOK] = jnp.where(col_io > row_io, turned, 0.0).astype(BF16)
+            toep[g, :, TOK : 2 * TOK] = jnp.where(col_io <= row_io, turned, 0.0).astype(BF16)
         return carry
 
-    lax.fori_loop(1, seq_n, send_mask, 0)
-
-    def build(g, carry):
-        base = jnp.broadcast_to(frev[pl.ds(g, 1), :], (TOK, TOK))
-        turned = pltpu.roll(base, 0, 1, stride=1, stride_axis=0)
-        toep[g, :, 0:TOK] = jnp.where(col_io > row_io, turned, 0.0).astype(BF16)
-        toep[g, :, TOK : 2 * TOK] = jnp.where(col_io <= row_io, turned, 0.0).astype(BF16)
-        return carry
-
-    lax.fori_loop(0, filt_ref.shape[0], build, 0)
+    lax.fori_loop(0, filt_ref.shape[0] // unroll, build, 0)
 
     halo.wait()
-    before = dot_rows(onehot(halo_tok), gate_tab[...])
+    before = dot(onehot(halo_tok), gate_tab[...])
     before = jnp.where(me > 0, before, 0.0).astype(BF16)
     for c in range(lane_tiles):
         for s in range(2):
@@ -386,7 +376,24 @@
     halves = [(n, s) for n in range(pairs) for s in range(2)]
     for n, s in halves:
         send_far(n, s)
-    ahead = 3
+
+    mask_own = pltpu.make_async_copy(mask_ref, mask_all.at[me], mask_r)
+    mask_own.start()
+
+    def send_mask(n, carry):
+        pltpu.make_async_remote_copy(
+            src_ref=mask_ref,
+            dst_ref=mask_all.at[me],
+            send_sem=mask_s,
+            recv_sem=mask_r,
+            device_id={"seq": peer(n)},
+            device_id_type=MESH,
+        ).start()
+        return carry
+
+    lax.fori_loop(1, seq_n, send_mask, 0)
+
+    ahead = len(halves)
     for n, s in halves[:ahead]:
         send_near(n, s)
         send_chain(n, s)

time: 61.4 us -> 54.2 us (0.88)
  Pallas kernels: 59.8 us -> 52.6 us
    pallas_call x1, Pallas kernels: 59.8 us -> 52.6 us  [body(): pl.pallas_call(functools.partial(kernel, seq_n, mp_n), out_shape=jax.Shap...]
where the time goes in v4:
time: 54.2 us; the launch traced here: 53.9 us
  Pallas kernels  52.6 us (97%)
  local copies, waits for them, and re-layouts  1.32 us (2%)
    pallas_call x1, Pallas kernels, body(): pl.pallas_call(functools.partial(kernel, seq_n, mp_n), out_shape=jax.Shap...  52.6 us
    unnamed x1, local copies, waits for them, and re-layouts  1.32 us

profile of v4, /device:TPU:1, one launch (start us, length us, event | category | flops | bytes accessed | tf_op | source)
XLA Modules:
  0.0 53.9 jit_solution(17963491179473017131)
XLA Ops:
  0.0 52.6 %steer.1 = f32[8,4,128]{2,1,0:T(4,128)} custom-call(s32[2,128]{1,0:T(2,128)} %tok_ref.1, s32[1,128]{1,0:T(1,128)} %bitcast.3, bf16[3,512,1024]{2,1,0:T(8,128)(2,1)} %bitcast.2, bf16[64,128]{1,0:T(8,128)(2,1)} %filt_ref.1, bf16[1024,4096]{1,0:T(8,128)(2,1)} %w_hbm.1, bf16[3,8,128,128]{3,2,1,0:T(8,128)(2,1)} %wqkv_hbm.1), custom_call_target="tpu_custom_call" | custom-call | tf_op jit(solution)/shard_map/steer/pallas_call | solution.py:570
  52.6 1.3 %copy.8 = f32[8,4,128]{2,1,0:T(4,128)} copy(f32[8,4,128]{2,1,0:T(4,128)} %steer.1) | data formatting | bytes 32768

commit v5 on v4

--- a/solution.py
+++ b/solution.py
@@ -170,6 +170,20 @@
             win[c, TOK : 2 * TOK, s * 128 : (s + 1) * 128] = current[
                 s * TOK : (s + 1) * TOK, c * 128 : (c + 1) * 128
             ]
+    unroll = 8
+
+    def build(step, carry):
+        for i in range(unroll):
+            g = step * unroll + i
+            base = jnp.broadcast_to(frev[pl.ds(g, 1), :], (TOK, TOK))
+            turned = pltpu.roll(base, 0, 1, stride=1, stride_axis=0)
+            toep[g, :, 0:TOK] = jnp.where(col_io > row_io, turned, 0.0).astype(BF16)
+            toep[g, :, TOK : 2 * TOK] = jnp.where(col_io <= row_io, turned, 0.0).astype(BF16)
+        return carry
+
+    build_steps = filt_ref.shape[0] // unroll
+    lax.fori_loop(0, build_steps // 2, build, 0)
+
     pl.semaphore_wait(barrier, seq_n + 1)
 
     halo = pltpu.make_async_remote_copy(
@@ -184,18 +198,7 @@
     for i in order:
         w_copies[i].start()
 
-    unroll = 8
-
-    def build(step, carry):
-        for i in range(unroll):
-            g = step * unroll + i
-            base = jnp.broadcast_to(frev[pl.ds(g, 1), :], (TOK, TOK))
-            turned = pltpu.roll(base, 0, 1, stride=1, stride_axis=0)
-            toep[g, :, 0:TOK] = jnp.where(col_io > row_io, turned, 0.0).astype(BF16)
-            toep[g, :, TOK : 2 * TOK] = jnp.where(col_io <= row_io, turned, 0.0).astype(BF16)
-        return carry
-
-    lax.fori_loop(0, filt_ref.shape[0] // unroll, build, 0)
+    lax.fori_loop(build_steps // 2, build_steps, build, 0)
 
     halo.wait()
     before = dot(onehot(halo_tok), gate_tab[...])

time: 54.2 us -> 54.5 us (level)
  no operation moved by 1% of the time
where the time goes in v5:
time: 54.5 us; the launch traced here: 54.2 us
  Pallas kernels  52.9 us (97%)
  local copies, waits for them, and re-layouts  1.32 us (2%)
    pallas_call x1, Pallas kernels, body(): pl.pallas_call(functools.partial(kernel, seq_n, mp_n), out_shape=jax.Shap...  52.9 us
    unnamed x1, local copies, waits for them, and re-layouts  1.32 us

profile of v5, /device:TPU:1, one launch (start us, length us, event | category | flops | bytes accessed | tf_op | source)
XLA Modules:
  0.0 54.2 jit_solution(8037952158375689609)
XLA Ops:
  0.0 52.9 %steer.1 = f32[8,4,128]{2,1,0:T(4,128)} custom-call(s32[2,128]{1,0:T(2,128)} %tok_ref.1, s32[1,128]{1,0:T(1,128)} %bitcast.3, bf16[3,512,1024]{2,1,0:T(8,128)(2,1)} %bitcast.2, bf16[64,128]{1,0:T(8,128)(2,1)} %filt_ref.1, bf16[1024,4096]{1,0:T(8,128)(2,1)} %w_hbm.1, bf16[3,8,128,128]{3,2,1,0:T(8,128)(2,1)} %wqkv_hbm.1), custom_call_target="tpu_custom_call" | custom-call | tf_op jit(solution)/shard_map/steer/pallas_call | solution.py:573
  52.9 1.3 %copy.8 = f32[8,4,128]{2,1,0:T(4,128)} copy(f32[8,4,128]{2,1,0:T(4,128)} %steer.1) | data formatting | bytes 32768
